TPU v7x, 32 devices: a whole 2x2x4 slice. The times are simulated.
32 devices in a mesh: grp: 2 (over y), pool: 4 (over z), tp: 2 (over x), sub: 2 (over core).
Axes of the slice: x: 2, y: 2, z: 4, core: 2. Of those that a mesh axis runs over, the one named last changes fastest.
Arguments:
- queries: bfloat16 [128, 4096], P(('grp', 'pool', 'tp', 'sub')), parts along dimension 0, may hold values from -48 to 48
- keys_cache: bfloat16 [128, 512, 256], P(('grp', 'pool', 'tp', 'sub')), parts along dimension 0, may hold values from -6 to 6
- values_cache: bfloat16 [128, 512, 256], P(('grp', 'pool', 'tp', 'sub')), parts along dimension 0, may hold values from -6 to 6
- lengths: int32 [128], P(('grp', 'pool', 'tp', 'sub')), parts along dimension 0, may hold values from 2 to 512
- out_weight: bfloat16 [4096, 2048], P(('tp', 'sub')), may hold values from -0.75 to 0.75
- routes: int32 [128, 8], P(('grp', 'pool')), parts along dimension 0, may hold values from 0 to 63, all different within a row; in each aligned block of 16 rows (0 to 15, 16 to 31, ...) at most 14 rows name the same one
- route_weight: float32 [128, 8], P(('grp', 'pool')), parts along dimension 0, may hold values from 0.1 to 0.5
- expert_table: int32 [64], replicated, may hold values from 0 to 63, each once
- w_gate: bfloat16 [64, 768, 2048], P('pool', 'sub', 'tp'), may hold values from -0.125 to 0.125
- w_up: bfloat16 [64, 768, 2048], P('pool', 'sub', 'tp'), may hold values from -0.125 to 0.125
- w_down: bfloat16 [64, 768, 2048], P('pool', 'sub', 'tp'), may hold values from -0.875 to 0.875
Outputs:
- attended: bfloat16 [128, 2048], P(('grp', 'pool', 'tp', 'sub')), parts along dimension 0
- expert_out: bfloat16 [128, 2048], P(('grp', 'pool'), ('tp', 'sub')), parts along dimension 0
There are 2 independent parts, one for each index of `grp`. A program takes and returns all parts, laid end to end along the dimension named above; an argument that names none is the same for every part. Nothing has to cross between parts.
Inputs may be any that keep to these rules, and one draw needn't show every extreme that they name: `routes`: in each aligned block of 16 rows (the rows of one pool index) no expert is named by more than 14 rows, and in some block one expert is named by exactly 14 rows; each row names 8 different experts. `expert_table`: a permutation of the experts.
All inputs are finite; a program needn't handle non-finite values.
Results may differ from a plain program's by a relative error of at most 0.0086.
Values may be sent and summed in bfloat16 or wider, within the bound.
No kernel may reach another device: no remote copies, remote signals or barrier semaphores. Data moves between devices by JAX's collectives and lax.ppermute only.
A program may use at most 128 MiB of HBM per device.

v0:
```python
import math
import jax
import jax.numpy as jnp
from jax import lax
from jax.sharding import PartitionSpec as P

D = 2048
HEADS = 32
KV_HEADS = 2
HEAD_DIM = 128
EXPERTS = 64
TOP_K = 8
CAPACITY = 14
masked_low = -1e30


def body(
    queries,
    keys_cache,
    values_cache,
    lengths,
    out_weight,
    routes,
    route_weight,
    expert_table,
    w_gate,
    w_up,
    w_down,
):
    shard_index = lax.axis_index(("tp", "sub"))
    pool_count = lax.axis_size("pool")
    tp_count = lax.axis_size("tp")
    tp_index = lax.axis_index("tp")
    sub_count = lax.axis_size("sub")
    sub_index = lax.axis_index("sub")
    row_count = queries.shape[0]
    positions = keys_cache.shape[1]
    group_size = HEADS // KV_HEADS
    query_four = queries.reshape(row_count, KV_HEADS, group_size, HEAD_DIM)
    key_four = keys_cache.reshape(row_count, positions, KV_HEADS, HEAD_DIM)
    value_four = values_cache.reshape(row_count, positions, KV_HEADS, HEAD_DIM)
    scores = jnp.einsum(
        "rkgd,rlkd->rkgl", query_four, key_four, preferred_element_type=jnp.float32
    ) * (1.0 / math.sqrt(HEAD_DIM))
    in_range = (lax.iota(jnp.int32, positions)[None, :] < lengths[:, None])[:, None, None, :]
    masked = jnp.where(in_range, scores, masked_low)
    row_max = jnp.max(masked, axis=3, keepdims=True)
    exp_terms = jnp.where(in_range, jnp.exp(masked - row_max), 0.0)
    exp_sum = jnp.sum(exp_terms, axis=3)
    weights = exp_terms.astype(jnp.bfloat16)
    weighted = jnp.einsum(
        "rkgl,rlkd->rkgd", weights, value_four, preferred_element_type=jnp.float32
    )
    attention = (
        (weighted / exp_sum[..., None]).reshape(row_count, HEADS * HEAD_DIM).astype(jnp.bfloat16)
    )
    head_rows = lax.all_to_all(attention, ("tp", "sub"), split_axis=1, concat_axis=0, tiled=True)
    partial_value = jnp.dot(head_rows, out_weight, preferred_element_type=jnp.float32)
    summed = lax.psum(partial_value, ("tp", "sub"))
    attended_all = summed.astype(jnp.bfloat16)
    attended = lax.dynamic_slice_in_dim(attended_all, shard_index * row_count, row_count, 0)
    pool_rows = attended_all.shape[0]
    pair_count = pool_rows * TOP_K
    expert_ids = lax.iota(jnp.int32, EXPERTS)
    flat_routes = routes.reshape(pair_count)
    entry_index = jnp.sum(
        jnp.where(flat_routes[:, None] == expert_ids[None, :], expert_table[None, :], 0), axis=1
    )
    entry_hot = (entry_index[:, None] == expert_ids[None, :]).astype(jnp.int32)
    slot_rank = jnp.sum((jnp.cumsum(entry_hot, axis=0) - entry_hot) * entry_hot, axis=1)
    slot_index = entry_index * CAPACITY + slot_rank
    slot_total = EXPERTS * CAPACITY
    slot_hot = (slot_index[:, None] == lax.iota(jnp.int32, slot_total)[None, :]).astype(
        jnp.bfloat16
    )
    row_hot = (
        (lax.iota(jnp.int32, pair_count) // TOP_K)[:, None]
        == lax.iota(jnp.int32, pool_rows)[None, :]
    ).astype(jnp.bfloat16)
    placing = jnp.einsum("ps,pr->sr", slot_hot, row_hot, preferred_element_type=jnp.float32).astype(
        jnp.bfloat16
    )
    outgoing = jnp.dot(placing, attended_all, preferred_element_type=jnp.float32).astype(
        jnp.bfloat16
    )
    outgoing = outgoing.reshape(pool_count, EXPERTS // pool_count, CAPACITY, D)
    block_width = D // tp_count
    half_width = block_width // sub_count
    own_slice = lax.dynamic_slice_in_dim(
        outgoing, tp_index * block_width + sub_index * half_width, half_width, 3
    )
    arrived = lax.all_to_all(own_slice, "pool", split_axis=0, concat_axis=0, tiled=True)
    incoming = lax.all_gather(arrived, "sub", axis=3, tiled=True)
    gate_part = jnp.einsum("pjcd,jfd->pjcf", incoming, w_gate, preferred_element_type=jnp.float32)
    up_part = jnp.einsum("pjcd,jfd->pjcf", incoming, w_up, preferred_element_type=jnp.float32)
    gate_value, up_value = lax.psum((gate_part, up_part), "tp")
    hidden = (jax.nn.silu(gate_value) * up_value).astype(jnp.bfloat16)
    partial_rows = jnp.einsum("pjcf,jfd->pjcd", hidden, w_down, preferred_element_type=jnp.float32)
    expert_rows = lax.psum_scatter(partial_rows, "sub", scatter_dimension=3, tiled=True).astype(
        jnp.bfloat16
    )
    returned = lax.all_to_all(expert_rows, "pool", split_axis=0, concat_axis=0, tiled=True)
    flat_back = returned.reshape(slot_total, returned.shape[3])
    picked = jnp.take(flat_back, slot_index, axis=0).astype(jnp.float32)
    scaled = picked * route_weight.reshape(pair_count)[:, None]
    expert_out = jnp.sum(scaled.reshape(pool_rows, TOP_K, returned.shape[3]), axis=1).astype(
        jnp.bfloat16
    )
    return (attended, expert_out)


def solution(mesh):
    in_specs = (
        P(("grp", "pool", "tp", "sub"), None),
        P(("grp", "pool", "tp", "sub"), None, None),
        P(("grp", "pool", "tp", "sub"), None, None),
        P(("grp", "pool", "tp", "sub")),
        P(("tp", "sub"), None),
        P(("grp", "pool"), None),
        P(("grp", "pool"), None),
        P(),
        P("pool", "sub", "tp"),
        P("pool", "sub", "tp"),
        P("pool", "sub", "tp"),
    )
    out_specs = (P(("grp", "pool", "tp", "sub"), None), P(("grp", "pool"), ("tp", "sub")))
    return jax.shard_map(body, mesh=mesh, in_specs=in_specs, out_specs=out_specs, check_vma=False)
```

profile of v0, /device:TPU:0, one launch (start us, length us, event | category | flops | bytes accessed | tf_op | source)
XLA Modules:
  0.0 255.0 jit_solution(3014672523360081864)
XLA Ops:
  7.2 0.8 copy.48
  8.1 0.7 iota_compare_fusion.8
  9.4 1.5 fusion.17
  11.6 4.2 %all-to-all-start = ((bf16[4,4,1024]{2,0,1:T(4,128)(2,1)}), bf16[4,4,1024]{2,0,1:T(4,128)(2,1)S(1)}, u32[]{:S(2)}, u32[]{:S(2)}) async-start(bf16[4,4,1024]{2,0,1:T(4,128)(2,1)} %copy.36), calls=%async_computation | async-start | bytes 65536 | tf_op jit(solution)/shard_map/all_to_all | solution.py:57
  16.6 3.1 %all-to-all-done = bf16[4,4,1024]{2,0,1:T(4,128)(2,1)S(1)} async-done(((bf16[4,4,1024]{2,0,1:T(4,128)(2,1)}), bf16[4,4,1024]{2,0,1:T(4,128)(2,1)S(1)}, u32[]{:S(2)}, u32[]{:S(2)}) %all-to-all-start) | async-done | bytes 32800 | tf_op jit(solution)/shard_map/all_to_all | solution.py:57
  19.7 2.8 %fusion.34 = f32[16,2048]{1,0:T(8,128)S(1)} fusion(bf16[16,1024]{1,0:T(8,128)(2,1)S(1)} %all_to_all.20, bf16[1024,2048]{1,0:T(8,128)(2,1)} %param.15), kind=kOutput, calls=%fused_computation.55 | convolution fusion | flops 67108864 | bytes 4358144 | tf_op jit(solution)/shard_map/dot_general | solution.py:58
  22.6 11.7 %all-reduce.5 = bf16[16,2048]{1,0:T(8,128)(2,1)S(1)} all-reduce(f32[16,2048]{1,0:T(8,128)S(1)} %fusion.34), channel_id=1, replica_groups=mesh['grp'=2,'pool'=4,'tp'=2,'sub'=2] {'tp','sub'}, use_global_device_ids=true, to_apply=%region_2.3 | all-reduce | flops 32768 | bytes 196608 | tf_op jit(solution)/shard_map/psum | solution.py:59
  34.3 3.2 %convolution_convert_fusion = bf16[896,2048]{1,0:T(8,128)(2,1)} fusion(bf16[16,2048]{1,0:T(8,128)(2,1)S(1)} %all-reduce.5, s32[128]{0:T(128)S(1)} %get-tuple-element.5, s32[128]{0:T(128)S(1)} %and_select_fusion), kind=kOutput, calls=%fused_computation.9 | convolution fusion | flops 64356352 | bytes 3736576 | tf_op jit(solution)/shard_map/dot_general | solution.py:83
  37.5 6.0 %reshape.116 = bf16[4,16,14,2048]{3,2,1,0:T(8,128)(2,1)} reshape(bf16[896,2048]{1,0:T(8,128)(2,1)} %convolution_convert_fusion) | data formatting | bytes 7340032 | tf_op jit(solution)/shard_map/reshape | solution.py:86
  43.5 1.3 constant_dynamic-slice_fusion
  45.4 28.3 %all_to_all.26 = bf16[4,16,14,512]{3,1,2,0:T(8,128)(2,1)S(1)} all-to-all(bf16[4,16,14,512]{3,1,2,0:T(8,128)(2,1)S(1)} %copy.38), channel_id=1, replica_groups=mesh['grp'=2,'pool'=4,'tp'=2,'sub'=2] {'pool'}, dimensions={0} | all-to-all | bytes 1835008 | tf_op jit(solution)/shard_map/all_to_all | solution.py:92
  73.7 1.5 copy.39
  75.3 8.9 %all-gather.2.cloned.1.call-done = bf16[4,16,14,1024]{3,2,0,1:T(8,128)(2,1)} async-done(((bf16[4,16,14,512]{3,2,0,1:T(8,128)(2,1)}), bf16[4,16,14,1024]{3,2,0,1:T(8,128)(2,1)}) %all-gather.2.cloned.1.call-update) | async-done | bytes 1835024 | tf_op jit(solution)/shard_map/all_gather | solution.py:93
  84.1 10.5 %fusion.10 = f32[4,16,14,384]{3,2,0,1:T(8,128)} fusion(bf16[4,16,14,1024]{3,2,0,1:T(8,128)(2,1)} %all-gather.2.cloned.1.call-done, bf16[16,384,1024]{2,1,0:T(8,128)(2,1)} %param.20), kind=kOutput, calls=%fused_computation.12 | convolution fusion | flops 704643072 | bytes 15794176 | tf_op jit(solution)/shard_map/pjcd,jfd->pjcf/dot_general | solution.py:95
  94.6 9.8 %fusion.7 = f32[4,16,14,384]{3,2,0,1:T(8,128)} fusion(bf16[4,16,14,1024]{3,2,0,1:T(8,128)(2,1)S(1)} %copy-done.2, bf16[16,384,1024]{2,1,0:T(8,128)(2,1)} %param.19), kind=kOutput, calls=%fused_computation.11 | convolution fusion | flops 704643072 | bytes 15794176 | tf_op jit(solution)/shard_map/pjcd,jfd->pjcf/dot_general | solution.py:94
  104.7 87.0 %all-reduce.4.cloned.1.call-done = (f32[4,16,14,384]{3,2,0,1:T(8,128)}, f32[4,16,14,384]{3,2,0,1:T(8,128)}) async-done(((f32[4,16,14,384]{3,2,0,1:T(8,128)}, f32[4,16,14,384]{3,2,0,1:T(8,128)}), (f32[4,16,14,384]{3,2,0,1:T(8,128)}, f32[4,16,14,384]{3,2,0,1:T(8,128)})) %all-reduce.4.cloned.1.call-update) | async-done | bytes 2752528 | tf_op jit(solution)/shard_map/psum | solution.py:96
  191.7 7.9 %fusion.1 = f32[16,4,14,1024]{3,2,1,0:T(8,128)S(1)} fusion(bf16[16,384,1024]{2,1,0:T(8,128)(2,1)} %param.21, f32[4,16,14,384]{3,2,0,1:T(8,128)} %get-tuple-element.2, f32[4,16,14,384]{3,2,0,1:T(8,128)} %get-tuple-element.3), kind=kOutput, calls=%fused_computation.2 | convolution fusion | flops 706707456 | bytes 19005440 | tf_op jit(solution)/shard_map/pjcf,jfd->pjcd/dot_general | solution.py:98
  199.6 3.9 %copy.58 = f32[16,4,14,1024]{3,0,2,1:T(8,128)} copy(f32[16,4,14,1024]{3,2,1,0:T(8,128)S(1)} %fusion.1) | data formatting | bytes 7340032 | tf_op jit(solution)/shard_map/pjcf,jfd->pjcd/dot_general | solution.py:98
  203.6 11.7 %reduce-scatter.2.cloned.1.call-done = f32[4,16,14,512]{3,1,2,0:T(8,128)} async-done(((f32[4,16,14,1024]{3,1,2,0:T(8,128)}), f32[4,16,14,512]{3,1,2,0:T(8,128)}) %reduce-scatter.2.cloned.1.call-update) | async-done | bytes 1835024 | tf_op jit(solution)/shard_map/reduce_scatter | solution.py:99
  215.3 2.6 %convert_element_type.45 = bf16[4,16,14,512]{3,1,2,0:T(8,128)(2,1)} convert(f32[4,16,14,512]{3,1,2,0:T(8,128)} %reduce-scatter.2.cloned.1.call-done) | non-fusion elementwise | flops 458752 | bytes 2752512 | tf_op jit(solution)/shard_map/convert_element_type | solution.py:99
  217.8 4.8 %all-to-all-start.2 = ((bf16[4,16,14,512]{3,1,2,0:T(8,128)(2,1)}), bf16[4,16,14,512]{3,1,2,0:T(8,128)(2,1)S(1)}, u32[]{:S(2)}, u32[]{:S(2)}) async-start(bf16[4,16,14,512]{3,1,2,0:T(8,128)(2,1)} %convert_element_type.45), calls=%async_computation.3 | async-start | bytes 1835008 | tf_op jit(solution)/shard_map/all_to_all | solution.py:102
  223.5 22.6 %all-to-all-done.2 = bf16[4,16,14,512]{3,1,2,0:T(8,128)(2,1)S(1)} async-done(((bf16[4,16,14,512]{3,1,2,0:T(8,128)(2,1)}), bf16[4,16,14,512]{3,1,2,0:T(8,128)(2,1)S(1)}, u32[]{:S(2)}, u32[]{:S(2)}) %all-to-all-start.2) | async-done | bytes 917536 | tf_op jit(solution)/shard_map/all_to_all | solution.py:102
  246.9 0.8 gather_fusion
  247.7 0.8 multiply_reduce_fusion
  (39 shorter events, 4.4 us)
Async XLA Ops:
  7.2 1.6 copy-start
  7.2 8.6 %copy-start.3 = (s32[16,8]{0,1:T(8,128)S(1)}, s32[16,8]{0,1:T(8,128)}, u32[]{:S(2)}) copy-start(s32[16,8]{0,1:T(8,128)} %param.16) | copy-start | bytes 1540
  7.2 8.8 %copy-start.5 = (s32[64]{0:T(128)S(1)}, s32[64]{0:T(128)}, u32[]{:S(2)}) copy-start(s32[64]{0:T(128)} %param.18) | copy-start | bytes 772
  11.6 8.2 %all-to-all-start = ((bf16[4,4,1024]{2,0,1:T(4,128)(2,1)}), bf16[4,4,1024]{2,0,1:T(4,128)(2,1)S(1)}, u32[]{:S(2)}, u32[]{:S(2)}) async-start(bf16[4,4,1024]{2,0,1:T(4,128)(2,1)} %copy.36), calls=%async_computation | async-start | bytes 65536 | tf_op jit(solution)/shard_map/all_to_all | solution.py:57
  15.8 68.3 %all-gather.2.cloned.1.call-start = ((), (), s32[]{:S(2)}) async-start(), calls=%async_computation.4 | async-start | bytes 3145728 | tf_op jit(solution)/shard_map/all_gather | solution.py:93
  75.2 116.5 %all-reduce.4.cloned.1.call-start = ((), (), s32[]{:S(2)}) async-start(), calls=%async_computation.6 | async-start | bytes 6291456 | tf_op jit(solution)/shard_map/psum | solution.py:96
  84.1 10.5 %copy-start.2 = (bf16[4,16,14,1024]{3,2,0,1:T(8,128)(2,1)S(1)}, bf16[4,16,14,1024]{3,2,0,1:T(8,128)(2,1)}, u32[]{:S(2)}) copy-start(bf16[4,16,14,1024]{3,2,0,1:T(8,128)(2,1)} %all-gather.2.cloned.1.call-done) | copy-start | bytes 5505028
  104.4 110.8 %reduce-scatter.2.cloned.1.call-start = ((), (), s32[]{:S(2)}) async-start(), calls=%async_computation.5 | async-start | bytes 5505024 | tf_op jit(solution)/shard_map/reduce_scatter | solution.py:99
  203.6 19.2 %copy-start.4 = (f32[16,8]{0,1:T(8,128)S(1)}, f32[16,8]{0,1:T(8,128)}, u32[]{:S(2)}) copy-start(f32[16,8]{0,1:T(8,128)} %param.17) | copy-start | bytes 1540
  217.8 28.2 %all-to-all-start.2 = ((bf16[4,16,14,512]{3,1,2,0:T(8,128)(2,1)}), bf16[4,16,14,512]{3,1,2,0:T(8,128)(2,1)S(1)}, u32[]{:S(2)}, u32[]{:S(2)}) async-start(bf16[4,16,14,512]{3,1,2,0:T(8,128)(2,1)} %convert_element_type.45), calls=%async_computation.3 | async-start | bytes 1835008 | tf_op jit(solution)/shard_map/all_to_all | solution.py:102
  246.1 2.4 copy-start.1
Sparse Core Ops, SparseCore 0:
  75.3 8.7 all-gather.1
  104.6 87.1 all-reduce.3
  203.7 11.5 reduce-scatter.1
where the time goes:
time: 256 us; the launch traced here: 255 us
  waiting for transfers between devices  133 us (52%)
  blocking collectives  40 us (16%)
  matrix products  36.2 us (14%)
  local copies, waits for them, and re-layouts  17.3 us (7%)
  between operations  13.9 us (5%)
  starting transfers between devices  9.29 us (4%)
  other arithmetic  4.91 us (2%)
    psum x1, waiting for transfers between devices, body(): gate_value, up_value = lax.psum((gate_part, up_part), 'tp')  87 us
    all_to_all x1, blocking collectives, body(): lax.all_to_all(own_slice, 'pool', split_axis=0, concat_axis=0, tiled=True)  28.3 us
    all_to_all x1, waiting for transfers between devices, body(): lax.all_to_all(expert_rows, 'pool', split_axis=0, concat_axis=0, tiled=True)  22.6 us
    psum x1, blocking collectives, body(): summed = lax.psum(partial_value, ('tp', 'sub'))  11.7 us
    reduce_scatter x1, waiting for transfers between devices, body(): lax.psum_scatter(partial_rows, 'sub', scatter_dimension=3, tiled=True)  11.7 us
    dot_general x1, matrix products, body(): jnp.einsum('pjcd,jfd->pjcf', incoming, w_up, preferred_element_type=jnp.f...  10.5 us
    dot_general x1, matrix products, body(): jnp.einsum('pjcd,jfd->pjcf', incoming, w_gate, preferred_element_type=jnp...  9.77 us
    all_gather x1, waiting for transfers between devices, body(): incoming = lax.all_gather(arrived, 'sub', axis=3, tiled=True)  8.87 us
  transfers between devices with their start and end apart: 5, of which 5 were waited for; matrix products, arithmetic and copies ran while one was open for 1% of the time, Pallas kernels for 0%

commit v1 on v0

--- a/solution.py
+++ b/solution.py
@@ -56,7 +56,8 @@
     )
     head_rows = lax.all_to_all(attention, ("tp", "sub"), split_axis=1, concat_axis=0, tiled=True)
     partial_value = jnp.dot(head_rows, out_weight, preferred_element_type=jnp.float32)
-    summed = lax.psum(partial_value, ("tp", "sub"))
+    inner = lax.psum(partial_value, "sub")
+    summed = lax.psum(inner, "tp")
     attended_all = summed.astype(jnp.bfloat16)
     attended = lax.dynamic_slice_in_dim(attended_all, shard_index * row_count, row_count, 0)
     pool_rows = attended_all.shape[0]

time: 256 us -> 272 us (1.062)
  waiting for transfers between devices: 133 us -> 152 us
  blocking collectives: 40 us -> 36.8 us
    psum x0 -> x1, waiting for transfers between devices: none -> 18.8 us  [body(): inner = lax.psum(partial_value, 'sub')]
  transfers between devices with their start and end apart: 5 -> 6, of which waited for: 5 -> 6; matrix products, arithmetic and copies ran while one was open for 1% -> 1% of each run, Pallas kernels for 0% -> 0%
where the time goes in v1:
time: 272 us; the launch traced here: 271 us
  waiting for transfers between devices  152 us (56%)
  matrix products  36.8 us (14%)
  blocking collectives  36.8 us (14%)
  local copies, waits for them, and re-layouts  17.3 us (6%)
  between operations  13.9 us (5%)
  starting transfers between devices  9.33 us (3%)
  other arithmetic  4.91 us (2%)
    psum x1, waiting for transfers between devices, body(): gate_value, up_value = lax.psum((gate_part, up_part), 'tp')  87 us
    all_to_all x1, blocking collectives, body(): lax.all_to_all(own_slice, 'pool', split_axis=0, concat_axis=0, tiled=True)  26.1 us
    all_to_all x1, waiting for transfers between devices, body(): lax.all_to_all(expert_rows, 'pool', split_axis=0, concat_axis=0, tiled=True)  22.6 us
    psum x1, waiting for transfers between devices, body(): inner = lax.psum(partial_value, 'sub')  18.8 us
    reduce_scatter x1, waiting for transfers between devices, body(): lax.psum_scatter(partial_rows, 'sub', scatter_dimension=3, tiled=True)  11.7 us
    psum x1, blocking collectives, body(): summed = lax.psum(inner, 'tp')  10.7 us
    dot_general x1, matrix products, body(): jnp.einsum('pjcd,jfd->pjcf', incoming, w_up, preferred_element_type=jnp.f...  10.5 us
    dot_general x1, matrix products, body(): jnp.einsum('pjcd,jfd->pjcf', incoming, w_gate, preferred_element_type=jnp...  9.77 us
  transfers between devices with their start and end apart: 6, of which 6 were waited for; matrix products, arithmetic and copies ran while one was open for 1% of the time, Pallas kernels for 0%

profile of v1, /device:TPU:0, one launch (start us, length us, event | category | flops | bytes accessed | tf_op | source)
XLA Modules:
  0.0 271.2 jit_solution(18326182148163177034)
XLA Ops:
  7.2 0.8 copy.48
  9.4 1.5 fusion.17
  11.6 4.2 %all-to-all-start = ((bf16[4,4,1024]{2,0,1:T(4,128)(2,1)}), bf16[4,4,1024]{2,0,1:T(4,128)(2,1)S(1)}, u32[]{:S(2)}, u32[]{:S(2)}) async-start(bf16[4,4,1024]{2,0,1:T(4,128)(2,1)} %copy.36), calls=%async_computation | async-start | bytes 65536 | tf_op jit(solution)/shard_map/all_to_all | solution.py:57
  16.6 3.1 %all-to-all-done = bf16[4,4,1024]{2,0,1:T(4,128)(2,1)S(1)} async-done(((bf16[4,4,1024]{2,0,1:T(4,128)(2,1)}), bf16[4,4,1024]{2,0,1:T(4,128)(2,1)S(1)}, u32[]{:S(2)}, u32[]{:S(2)}) %all-to-all-start) | async-done | bytes 32800 | tf_op jit(solution)/shard_map/all_to_all | solution.py:57
  19.7 3.5 %fusion.34 = f32[16,2048]{1,0:T(8,128)} fusion(bf16[16,1024]{1,0:T(8,128)(2,1)S(1)} %all_to_all.20, bf16[1024,2048]{1,0:T(8,128)(2,1)} %param.15), kind=kOutput, calls=%fused_computation.55 | convolution fusion | flops 67108864 | bytes 4358144 | tf_op jit(solution)/shard_map/dot_general | solution.py:58
  23.4 18.8 %all-reduce.5.cloned.1.call-done = f32[16,2048]{1,0:T(8,128)} async-done(((f32[16,2048]{1,0:T(8,128)}), f32[16,2048]{1,0:T(8,128)}) %all-reduce.5.cloned.1.call-update) | async-done | bytes 131088 | tf_op jit(solution)/shard_map/psum | solution.py:59
  42.1 10.7 %all-reduce.8 = bf16[16,2048]{1,0:T(8,128)(2,1)S(1)} all-reduce(f32[16,2048]{1,0:T(8,128)} %all-reduce.5.cloned.1.call-done), channel_id=1, replica_groups=mesh['grp'=2,'pool'=4,'tp'=2,'sub'=2] {'tp'}, use_global_device_ids=true, to_apply=%region_3.4 | all-reduce | flops 32768 | bytes 196608 | tf_op jit(solution)/shard_map/psum | solution.py:60
  52.8 3.2 %convolution_convert_fusion = bf16[896,2048]{1,0:T(8,128)(2,1)} fusion(bf16[16,2048]{1,0:T(8,128)(2,1)S(1)} %all-reduce.8, s32[128]{0:T(128)S(1)} %get-tuple-element.5, s32[128]{0:T(128)S(1)} %and_select_fusion), kind=kOutput, calls=%fused_computation.9 | convolution fusion | flops 64356352 | bytes 3736576 | tf_op jit(solution)/shard_map/dot_general | solution.py:84
  56.0 6.0 %reshape.116 = bf16[4,16,14,2048]{3,2,1,0:T(8,128)(2,1)} reshape(bf16[896,2048]{1,0:T(8,128)(2,1)} %convolution_convert_fusion) | data formatting | bytes 7340032 | tf_op jit(solution)/shard_map/reshape | solution.py:87
  62.0 1.3 constant_dynamic-slice_fusion
  63.9 26.1 %all_to_all.26 = bf16[4,16,14,512]{3,1,2,0:T(8,128)(2,1)S(1)} all-to-all(bf16[4,16,14,512]{3,1,2,0:T(8,128)(2,1)S(1)} %copy.38), channel_id=1, replica_groups=mesh['grp'=2,'pool'=4,'tp'=2,'sub'=2] {'pool'}, dimensions={0} | all-to-all | bytes 1835008 | tf_op jit(solution)/shard_map/all_to_all | solution.py:93
  90.0 1.5 copy.39
  91.5 8.8 %all-gather.2.cloned.1.call-done = bf16[4,16,14,1024]{3,2,0,1:T(8,128)(2,1)} async-done(((bf16[4,16,14,512]{3,2,0,1:T(8,128)(2,1)}), bf16[4,16,14,1024]{3,2,0,1:T(8,128)(2,1)}) %all-gather.2.cloned.1.call-update) | async-done | bytes 1835024 | tf_op jit(solution)/shard_map/all_gather | solution.py:94
  100.3 10.5 %fusion.10 = f32[4,16,14,384]{3,2,0,1:T(8,128)} fusion(bf16[4,16,14,1024]{3,2,0,1:T(8,128)(2,1)} %all-gather.2.cloned.1.call-done, bf16[16,384,1024]{2,1,0:T(8,128)(2,1)} %param.20), kind=kOutput, calls=%fused_computation.12 | convolution fusion | flops 704643072 | bytes 15794176 | tf_op jit(solution)/shard_map/pjcd,jfd->pjcf/dot_general | solution.py:96
  110.9 9.8 %fusion.7 = f32[4,16,14,384]{3,2,0,1:T(8,128)} fusion(bf16[4,16,14,1024]{3,2,0,1:T(8,128)(2,1)S(1)} %copy-done.2, bf16[16,384,1024]{2,1,0:T(8,128)(2,1)} %param.19), kind=kOutput, calls=%fused_computation.11 | convolution fusion | flops 704643072 | bytes 15794176 | tf_op jit(solution)/shard_map/pjcd,jfd->pjcf/dot_general | solution.py:95
  120.9 87.0 %all-reduce.7.cloned.1.call-done = (f32[4,16,14,384]{3,2,0,1:T(8,128)}, f32[4,16,14,384]{3,2,0,1:T(8,128)}) async-done(((f32[4,16,14,384]{3,2,0,1:T(8,128)}, f32[4,16,14,384]{3,2,0,1:T(8,128)}), (f32[4,16,14,384]{3,2,0,1:T(8,128)}, f32[4,16,14,384]{3,2,0,1:T(8,128)})) %all-reduce.7.cloned.1.call-update) | async-done | bytes 2752528 | tf_op jit(solution)/shard_map/psum | solution.py:97
  207.9 7.9 %fusion.1 = f32[16,4,14,1024]{3,2,1,0:T(8,128)S(1)} fusion(bf16[16,384,1024]{2,1,0:T(8,128)(2,1)} %param.21, f32[4,16,14,384]{3,2,0,1:T(8,128)} %get-tuple-element.2, f32[4,16,14,384]{3,2,0,1:T(8,128)} %get-tuple-element.3), kind=kOutput, calls=%fused_computation.2 | convolution fusion | flops 706707456 | bytes 19005440 | tf_op jit(solution)/shard_map/pjcf,jfd->pjcd/dot_general | solution.py:99
  215.8 3.9 %copy.58 = f32[16,4,14,1024]{3,0,2,1:T(8,128)} copy(f32[16,4,14,1024]{3,2,1,0:T(8,128)S(1)} %fusion.1) | data formatting | bytes 7340032 | tf_op jit(solution)/shard_map/pjcf,jfd->pjcd/dot_general | solution.py:99
  219.8 11.7 %reduce-scatter.2.cloned.1.call-done = f32[4,16,14,512]{3,1,2,0:T(8,128)} async-done(((f32[4,16,14,1024]{3,1,2,0:T(8,128)}), f32[4,16,14,512]{3,1,2,0:T(8,128)}) %reduce-scatter.2.cloned.1.call-update) | async-done | bytes 1835024 | tf_op jit(solution)/shard_map/reduce_scatter | solution.py:100
  231.5 2.6 convert_element_type.45
  234.1 4.8 %all-to-all-start.2 = ((bf16[4,16,14,512]{3,1,2,0:T(8,128)(2,1)}), bf16[4,16,14,512]{3,1,2,0:T(8,128)(2,1)S(1)}, u32[]{:S(2)}, u32[]{:S(2)}) async-start(bf16[4,16,14,512]{3,1,2,0:T(8,128)(2,1)} %convert_element_type.45), calls=%async_computation.3 | async-start | bytes 1835008 | tf_op jit(solution)/shard_map/all_to_all | solution.py:103
  239.7 22.6 %all-to-all-done.2 = bf16[4,16,14,512]{3,1,2,0:T(8,128)(2,1)S(1)} async-done(((bf16[4,16,14,512]{3,1,2,0:T(8,128)(2,1)}), bf16[4,16,14,512]{3,1,2,0:T(8,128)(2,1)S(1)}, u32[]{:S(2)}, u32[]{:S(2)}) %all-to-all-start.2) | async-done | bytes 917536 | tf_op jit(solution)/shard_map/all_to_all | solution.py:103
  263.1 0.8 gather_fusion
  263.9 0.8 multiply_reduce_fusion
  (42 shorter events, 5.2 us)
Async XLA Ops:
  7.2 1.6 copy-start
  7.2 8.6 %copy-start.3 = (s32[16,8]{0,1:T(8,128)S(1)}, s32[16,8]{0,1:T(8,128)}, u32[]{:S(2)}) copy-start(s32[16,8]{0,1:T(8,128)} %param.16) | copy-start | bytes 1540
  7.2 8.8 %copy-start.5 = (s32[64]{0:T(128)S(1)}, s32[64]{0:T(128)}, u32[]{:S(2)}) copy-start(s32[64]{0:T(128)} %param.18) | copy-start | bytes 772
  11.6 8.2 %all-to-all-start = ((bf16[4,4,1024]{2,0,1:T(4,128)(2,1)}), bf16[4,4,1024]{2,0,1:T(4,128)(2,1)S(1)}, u32[]{:S(2)}, u32[]{:S(2)}) async-start(bf16[4,4,1024]{2,0,1:T(4,128)(2,1)} %copy.36), calls=%async_computation | async-start | bytes 65536 | tf_op jit(solution)/shard_map/all_to_all | solution.py:57
  15.8 26.4 %all-reduce.5.cloned.1.call-start = ((), (), s32[]{:S(2)}) async-start(), calls=%async_computation.4 | async-start | bytes 262144 | tf_op jit(solution)/shard_map/psum | solution.py:59
  23.3 77.1 %all-gather.2.cloned.1.call-start = ((), (), s32[]{:S(2)}) async-start(), calls=%async_computation.5 | async-start | bytes 3145728 | tf_op jit(solution)/shard_map/all_gather | solution.py:94
  91.5 116.4 %all-reduce.7.cloned.1.call-start = ((), (), s32[]{:S(2)}) async-start(), calls=%async_computation.7 | async-start | bytes 6291456 | tf_op jit(solution)/shard_map/psum | solution.py:97
  100.3 10.5 %copy-start.2 = (bf16[4,16,14,1024]{3,2,0,1:T(8,128)(2,1)S(1)}, bf16[4,16,14,1024]{3,2,0,1:T(8,128)(2,1)}, u32[]{:S(2)}) copy-start(bf16[4,16,14,1024]{3,2,0,1:T(8,128)(2,1)} %all-gather.2.cloned.1.call-done) | copy-start | bytes 5505028
  120.6 110.8 %reduce-scatter.2.cloned.1.call-start = ((), (), s32[]{:S(2)}) async-start(), calls=%async_computation.6 | async-start | bytes 5505024 | tf_op jit(solution)/shard_map/reduce_scatter | solution.py:100
  219.8 19.2 %copy-start.4 = (f32[16,8]{0,1:T(8,128)S(1)}, f32[16,8]{0,1:T(8,128)}, u32[]{:S(2)}) copy-start(f32[16,8]{0,1:T(8,128)} %param.17) | copy-start | bytes 1540
  234.1 28.2 %all-to-all-start.2 = ((bf16[4,16,14,512]{3,1,2,0:T(8,128)(2,1)}), bf16[4,16,14,512]{3,1,2,0:T(8,128)(2,1)S(1)}, u32[]{:S(2)}, u32[]{:S(2)}) async-start(bf16[4,16,14,512]{3,1,2,0:T(8,128)(2,1)} %convert_element_type.45), calls=%async_computation.3 | async-start | bytes 1835008 | tf_op jit(solution)/shard_map/all_to_all | solution.py:103
  262.3 2.4 copy-start.1
Sparse Core Ops, SparseCore 0:
  23.4 18.6 all-reduce.4
  91.6 8.6 all-gather.1
  120.8 87.1 all-reduce.6
  219.9 11.5 reduce-scatter.1
